TPU v7x, 256 devices: a whole 4x4x8 slice. The times are simulated.
256 devices in a mesh: req: 32 (over z, y), mdl: 8 (over x, core).
Axes of the slice: x: 4, y: 4, z: 8, core: 2. Of those that a mesh axis runs over, the one named last changes fastest.
Arguments:
- tokens: bfloat16 [8192, 2048], P('req', 'mdl'), may hold values from -6 to 6
- prefix_cache: bfloat16 [16384, 2, 2048], P('req', None, 'mdl'), may hold values from -68 to 68
- qkv_weight: bfloat16 [2048, 3, 2048], P(None, None, 'mdl'), may hold values from -0.125 to 0.125
- out_weight: bfloat16 [2048, 2048], P('mdl'), may hold values from -0.75 to 0.75
- gate_up_weight: bfloat16 [2048, 2, 4096], P(None, None, 'mdl'), may hold values from -0.125 to 0.125
- down_weight: bfloat16 [4096, 2048], P('mdl'), may hold values from -0.09375 to 0.09375
- lengths: int32 [128], replicated, may hold values from 0 to 256, as said below
- placement: int32 [128], replicated, may hold values from 0 to 31, as said below
- request_group: int32 [128], replicated, may hold values from 0 to 3
- block_owner: int32 [32], replicated, may hold values from 0 to 31, each once
- start_position: int32 [128], replicated, may hold values from 4096 to 4351
Outputs:
- out: bfloat16 [8192, 2048], P('req', 'mdl')
Inputs may be any that keep to these rules, and one draw needn't show every extreme that they name: `placement`: each index of req holds exactly 4 requests. The lengths of the requests on one index of req sum to at most 256, and to exactly 256 on some index; all lengths together sum to exactly 128 times the number of indices of req.
All inputs are finite; a program needn't handle non-finite values.
Results may differ from a plain program's by a relative error of at most 0.017.
Values may be sent and summed in bfloat16 or wider, within the bound.
A program may use at most 128 MiB of HBM per device.

v0:
```python
import math
import jax
import jax.numpy as jnp
from jax import lax
from jax.sharding import PartitionSpec as P

HD = 128
G = 4
NEG = -1e30
EPS = 1e-05


def slot_table(lengths, placement, request_group, start_position, device, capacity):
    request_count = lengths.shape[0]
    request_ids = jnp.arange(request_count, dtype=jnp.int32)
    same_device = placement[:, None] == placement[None, :]
    earlier = request_ids[None, :] < request_ids[:, None]
    before = jnp.sum(jnp.where(same_device & earlier, lengths[None, :], 0), axis=1)
    ending = before + lengths
    slot_ids = jnp.arange(capacity, dtype=jnp.int32)
    belongs = (
        (placement[None, :] == device)
        & (slot_ids[:, None] >= before[None, :])
        & (slot_ids[:, None] < ending[None, :])
    )
    occupied = jnp.any(belongs, axis=1)
    request = jnp.sum(jnp.where(belongs, request_ids[None, :], 0), axis=1)
    slot_group = jnp.where(
        occupied, jnp.sum(jnp.where(belongs, request_group[None, :], 0), axis=1), -1
    )
    first_slot = jnp.sum(jnp.where(belongs, before[None, :], 0), axis=1)
    offset = slot_ids - first_slot
    position = jnp.sum(jnp.where(belongs, start_position[None, :], 0), axis=1) + offset
    return (occupied, request, slot_group, offset, position)


def block_groups(block_owner, group_count):
    block_count = block_owner.shape[0]
    per_group = block_count // group_count
    entry_ids = jnp.arange(block_count, dtype=jnp.int32)
    hits = block_owner[None, :] == entry_ids[:, None]
    entry = jnp.sum(jnp.where(hits, entry_ids[None, :], 0), axis=1)
    return entry // per_group


def lookup(values, wanted):
    hits = jnp.arange(values.shape[0], dtype=jnp.int32) == wanted
    return jnp.sum(jnp.where(hits, values, 0))


def rotate(vectors, position):
    half_width = vectors.shape[-1] // 2
    pair_ids = jnp.arange(half_width, dtype=jnp.float32)
    frequency = jnp.exp(pair_ids * (-2.0 * math.log(10000.0) / vectors.shape[-1]))
    angles = position.astype(jnp.float32)[:, None] * frequency[None, :]
    cosine = jnp.cos(angles)[:, None, :]
    sine_part = jnp.sin(angles)[:, None, :]
    lower = vectors[..., :half_width]
    upper = vectors[..., half_width:]
    return jnp.concatenate(
        [lower * cosine - upper * sine_part, upper * cosine + lower * sine_part], axis=-1
    )


def layer_norm(values):
    row_mean = jnp.mean(values, axis=-1, keepdims=True)
    centered = values - row_mean
    row_var = jnp.mean(centered * centered, axis=-1, keepdims=True)
    return centered * lax.rsqrt(row_var + EPS)


def block_partial(queries, key_rows, value_rows, allowed):
    score_scale = queries.shape[-1] ** (-0.5)
    scores = (
        jnp.einsum("shd,khd->hsk", queries, key_rows, preferred_element_type=jnp.float32)
        * score_scale
    )
    scores = jnp.where(allowed[None], scores, NEG)
    row_max = jnp.max(scores, axis=-1)
    weights = jnp.where(allowed[None], jnp.exp(scores - row_max[..., None]), 0.0)
    weight_sum = jnp.sum(weights, axis=-1)
    present = jnp.any(allowed, axis=-1)[None, :]
    safe_sum = jnp.where(present, weight_sum, 1.0)
    mixture = jnp.einsum(
        "hsk,khd->shd", weights.astype(jnp.bfloat16), value_rows, preferred_element_type=jnp.float32
    )
    normalized = (mixture / jnp.transpose(safe_sum)[:, :, None]).astype(jnp.bfloat16)
    log_sum = jnp.where(present, row_max + jnp.log(safe_sum), NEG)
    return (normalized, jnp.transpose(log_sum))


def combine(merged, partial_out, partial_lse):
    weighted, running_max, weight_sum = merged
    new_max = jnp.maximum(running_max, partial_lse)
    old_scale = jnp.exp(running_max - new_max)
    new_scale = jnp.exp(partial_lse - new_max)
    weighted = (
        weighted * old_scale[..., None] + partial_out.astype(jnp.float32) * new_scale[..., None]
    )
    return (weighted, new_max, weight_sum * old_scale + new_scale)


def feed_forward(residual_rows, gate_up_weight, down_weight):
    full_rows = lax.all_gather(residual_rows, "mdl", axis=1, tiled=True)
    normed = layer_norm(full_rows.astype(jnp.float32)).astype(jnp.bfloat16)
    gate_up = jnp.einsum("sd,dtf->stf", normed, gate_up_weight, preferred_element_type=jnp.float32)
    hidden = (jax.nn.silu(gate_up[:, 0]) * gate_up[:, 1]).astype(jnp.bfloat16)
    partial_sums = jnp.dot(hidden, down_weight, preferred_element_type=jnp.float32)
    return lax.psum_scatter(
        partial_sums.astype(jnp.bfloat16), "mdl", scatter_dimension=1, tiled=True
    ).astype(jnp.float32)


def local(
    tokens,
    prefix_cache,
    qkv_weight,
    out_weight,
    gate_up_weight,
    down_weight,
    lengths,
    placement,
    request_group,
    block_owner,
    start_position,
):
    capacity = tokens.shape[0]
    head_width = out_weight.shape[0]
    head_count = head_width // HD
    block_rows = prefix_cache.shape[0]
    device = lax.axis_index("req")
    occupied, request, slot_group, offset, position = slot_table(
        lengths, placement, request_group, start_position, device, capacity
    )
    gathered = lax.all_gather(tokens, "mdl", axis=1, tiled=True)
    normed = layer_norm(gathered.astype(jnp.float32)).astype(jnp.bfloat16)
    projected = jnp.einsum("sd,dtc->stc", normed, qkv_weight, preferred_element_type=jnp.float32)
    queries = rotate(projected[:, 0].reshape(capacity, head_count, HD), position).astype(
        jnp.bfloat16
    )
    key_rows = rotate(projected[:, 1].reshape(capacity, head_count, HD), position).astype(
        jnp.bfloat16
    )
    value_rows = projected[:, 2].reshape(capacity, head_count, HD).astype(jnp.bfloat16)
    group_table = block_groups(block_owner, G)
    start_state = (
        jnp.zeros((capacity, head_count, HD), jnp.float32),
        jnp.full((capacity, head_count), NEG, jnp.float32),
        jnp.zeros((capacity, head_count), jnp.float32),
    )
    merged = start_state
    arrived = lax.all_gather(prefix_cache, "req", axis=0, tiled=True)
    block_count = arrived.shape[0] // block_rows
    blocks = arrived.reshape(block_count, block_rows, 2, head_count, HD)

    def over_blocks(running, element):
        block, block_index = element
        block_group = lookup(group_table, block_index)
        allowed = jnp.broadcast_to((slot_group == block_group)[:, None], (capacity, block_rows))
        partial_out, partial_lse = block_partial(queries, block[:, 0], block[:, 1], allowed)
        return (combine(running, partial_out, partial_lse), None)

    merged, unused = lax.scan(
        over_blocks, merged, (blocks, jnp.arange(block_count, dtype=jnp.int32))
    )
    causal = (
        occupied[:, None]
        & occupied[None, :]
        & (request[:, None] == request[None, :])
        & (offset[None, :] <= offset[:, None])
    )
    partial_out, partial_lse = block_partial(queries, key_rows, value_rows, causal)
    weighted, running_max, weight_sum = combine(merged, partial_out, partial_lse)
    attention = (
        (weighted / weight_sum[..., None]).reshape(capacity, head_width).astype(jnp.bfloat16)
    )
    head_terms = jnp.dot(attention, out_weight, preferred_element_type=jnp.float32)
    residual = (
        tokens.astype(jnp.float32)
        + lax.psum_scatter(
            head_terms.astype(jnp.bfloat16), "mdl", scatter_dimension=1, tiled=True
        ).astype(jnp.float32)
    ).astype(jnp.bfloat16)
    finished = residual.astype(jnp.float32) + feed_forward(residual, gate_up_weight, down_weight)
    return jnp.where(occupied[:, None], finished, 0.0).astype(jnp.bfloat16)


def solution(mesh):
    in_specs = (
        P("req", "mdl"),
        P("req", None, "mdl"),
        P(None, None, "mdl"),
        P("mdl", None),
        P(None, None, "mdl"),
        P("mdl", None),
        P(),
        P(),
        P(),
        P(),
        P(),
    )
    out_specs = P("req", "mdl")
    return jax.shard_map(local, mesh=mesh, in_specs=in_specs, out_specs=out_specs, check_vma=False)
```

profile of v0, /device:TPU:8, one launch (start us, length us, event | category | flops | bytes accessed | tf_op | source)
XLA Modules:
  0.0 526.2 jit_solution(17898964725796724855)
XLA Ops:
  15.4 22.5 %all-gather.6.cloned.1.call-done = bf16[256,2048]{1,0:T(8,128)(2,1)} async-done(((bf16[256,256]{1,0:T(8,128)(2,1)}), bf16[256,2048]{1,0:T(8,128)(2,1)}) %all-gather.6.cloned.1.call-update) | async-done | bytes 1048592 | tf_op jit(solution)/shard_map/all_gather | solution.py:135
  38.0 1.5 convert_reduce_fusion.1
  39.5 1.6 fusion.26
  41.2 1.5 fusion.37
  45.9 1.7 fusion.75
  47.6 1.7 copy.66
  49.3 1.7 copy.67
  51.0 1.7 copy.65
  57.2 123.7 %all-gather.4.cloned.1.call-done = bf16[16384,2,256]{2,1,0:T(2,128)(2,1)} async-done(((bf16[512,2,256]{2,1,0:T(2,128)(2,1)}), bf16[16384,2,256]{2,1,0:T(2,128)(2,1)}) %all-gather.4.cloned.1.call-update) | async-done | bytes 16777232 | tf_op jit(solution)/shard_map/all_gather | solution.py:152
  180.9 41.4 %reshape.208 = bf16[32,512,2,2,128]{4,3,2,1,0:T(2,128)(2,1)} reshape(bf16[16384,2,256]{2,1,0:T(2,128)(2,1)} %all-gather.4.cloned.1.call-done) | data formatting | bytes 33554432 | tf_op jit(solution)/shard_map/reshape | solution.py:154
  222.4 188.9 %while.15 = (s32[]{:T(128)}, f32[256,2,128]{0,2,1:T(8,128)}, f32[256,2]{0,1:T(2,128)S(1)}, f32[256,2]{0,1:T(2,128)S(1)}, s32[32]{0:T(128)S(1)}, /*index=5*/s32[3...) while((s32[]{:T(128)}, f32[256,2,128]{0,2,1:T(8,128)}, ...), condition=%wide.region_13.14_spmd.clone, body=%wide.region_8.0_spmd.clone.sunk | while | flops 137171552 | bytes 8558420 | solution.py:163
  225.1 1.5 constant_dynamic-slice_fusion.2
  231.0 1.5 constant_dynamic-slice_fusion.2
  236.9 1.5 constant_dynamic-slice_fusion.2
  242.9 1.5 constant_dynamic-slice_fusion.2
  248.8 1.5 constant_dynamic-slice_fusion.2
  254.7 1.5 constant_dynamic-slice_fusion.2
  266.5 1.5 constant_dynamic-slice_fusion.2
  272.4 1.5 constant_dynamic-slice_fusion.2
  278.3 1.5 constant_dynamic-slice_fusion.2
  284.2 1.5 constant_dynamic-slice_fusion.2
  290.1 1.5 constant_dynamic-slice_fusion.2
  296.0 1.5 constant_dynamic-slice_fusion.2
  414.4 32.8 %reduce-scatter.3.cloned.1.call-done = bf16[256,256]{1,0:T(8,128)(2,1)} async-done(((bf16[256,2048]{1,0:T(8,128)(2,1)}), bf16[256,256]{1,0:T(8,128)(2,1)}) %reduce-scatter.3.cloned.1.call-update) | async-done | bytes 131088 | tf_op jit(solution)/shard_map/reduce_scatter | solution.py:180
  447.2 1.6 add_convert_fusion
  448.9 24.9 %all-gather.8.cloned.1.call-done = bf16[256,2048]{1,0:T(8,128)(2,1)} async-done(((bf16[256,256]{1,0:T(8,128)(2,1)}), bf16[256,2048]{1,0:T(8,128)(2,1)}) %all-gather.8.cloned.1.call-update) | async-done | bytes 1048592 | tf_op jit(solution)/shard_map/all_gather | solution.py:104
  473.7 1.5 convert_reduce_fusion
  475.3 1.6 fusion.24
  476.9 3.7 fusion.18
  480.6 1.7 convolution_convert_fusion
  482.4 35.6 %reduce-scatter.5.cloned.1.call-done = bf16[256,256]{1,0:T(8,128)(2,1)} async-done(((bf16[256,2048]{1,0:T(8,128)(2,1)}), bf16[256,256]{1,0:T(8,128)(2,1)}) %reduce-scatter.5.cloned.1.call-update) | async-done | bytes 131088 | tf_op jit(solution)/shard_map/reduce_scatter | solution.py:109
  518.0 1.7 select_convert_fusion
  (537 shorter events, 189.1 us)
Async XLA Ops:
  6.5 34.6 %copy-start = (bf16[2048,3,256]{2,0,1:T(8,128)(2,1)S(1)}, bf16[2048,3,256]{2,0,1:T(8,128)(2,1)}, u32[]{:S(2)}) copy-start(bf16[2048,3,256]{2,0,1:T(8,128)(2,1)} %param.15) | copy-start | bytes 9437188
  6.5 31.4 %all-gather.6.cloned.1.call-start = ((), (), s32[]{:S(2)}) async-start(), calls=%async_computation.3 | async-start | bytes 1179648 | tf_op jit(solution)/shard_map/all_gather | solution.py:135
  7.3 173.7 %all-gather.4.cloned.1.call-start = ((), (), s32[]{:S(2)}) async-start(), calls=%async_computation.2 | async-start | bytes 17301504 | tf_op jit(solution)/shard_map/all_gather | solution.py:152
  8.0 439.2 %reduce-scatter.3.cloned.1.call-start = ((), (), s32[]{:S(2)}) async-start(), calls=%async_computation.4 | async-start | bytes 1179648 | tf_op jit(solution)/shard_map/reduce_scatter | solution.py:180
  38.0 3.2 copy-start.1
  52.8 4.4 copy-start.9
  57.2 165.1 %copy-start.14 = (s32[32]{0:T(128)S(1)}, s32[32]{0:T(128)}, u32[]{:S(2)}) copy-start(s32[32]{0:T(128)} %and_select_fusion) | copy-start | bytes 388
  222.4 189.0 %copy-start.10 = (pred[256]{0:T(512)(128)(4,1)S(1)}, pred[256]{0:T(512)(128)(4,1)}, u32[]{:S(2)}) copy-start(pred[256]{0:T(512)(128)(4,1)} %get-tuple-element.157) | copy-start | bytes 772
  222.4 189.0 %copy-start.6 = (pred[256,256]{0,1:T(8,128)(4,1)S(1)}, pred[256,256]{0,1:T(8,128)(4,1)}, u32[]{:S(2)}) copy-start(pred[256,256]{0,1:T(8,128)(4,1)} %copy.53) | copy-start | bytes 196612
  222.4 189.0 %copy-start.8 = (bf16[256,1,256]{0,2,1:T(8,128)(2,1)S(1)}, bf16[256,1,256]{0,2,1:T(8,128)(2,1)}, u32[]{:S(2)}) copy-start(bf16[256,1,256]{0,2,1:T(8,128)(2,1)} %slice.71) | copy-start | bytes 393220
  225.1 2.1 copy-start.12
  231.0 2.1 copy-start.12
  236.9 2.1 copy-start.12
  242.8 2.1 copy-start.12
  266.5 2.1 copy-start.12
  272.4 2.1 copy-start.12
  278.3 2.1 copy-start.12
  284.2 2.1 copy-start.12
  290.1 2.1 copy-start.12
  296.0 2.1 copy-start.12
  301.9 2.1 copy-start.12
  319.6 2.1 copy-start.12
  325.5 2.1 copy-start.12
  331.4 2.1 copy-start.12
  337.3 2.1 copy-start.12
  343.2 2.1 copy-start.12
  412.8 34.4 %copy-start.7 = (bf16[256,256]{1,0:T(8,128)(2,1)S(1)}, bf16[256,256]{1,0:T(8,128)(2,1)}, u32[]{:S(2)}) copy-start(bf16[256,256]{1,0:T(8,128)(2,1)} %param.13) | copy-start | bytes 393220
  414.3 59.4 %all-gather.8.cloned.1.call-start = ((), (), s32[]{:S(2)}) async-start(), calls=%async_computation.5 | async-start | bytes 1179648 | tf_op jit(solution)/shard_map/all_gather | solution.py:104
  448.8 69.2 %reduce-scatter.5.cloned.1.call-start = ((), (), s32[]{:S(2)}) async-start(), calls=%async_computation.6 | async-start | bytes 1179648 | tf_op jit(solution)/shard_map/reduce_scatter | solution.py:109
  473.7 3.2 copy-start.2
  476.9 3.7 copy-start.11
  480.6 37.4 %copy-start.4 = (bf16[256,256]{1,0:T(8,128)(2,1)S(1)}, bf16[256,256]{1,0:T(8,128)(2,1)}, u32[]{:S(2)}) copy-start(bf16[256,256]{1,0:T(8,128)(2,1)} %add_convert_fusion) | copy-start | bytes 393220
  (50 other events, 58.0 us)
Sparse Core Ops, SparseCore 0:
  9.2 28.7 all-gather.5
  40.6 140.3 all-gather.3
  414.4 32.7 reduce-scatter.2
  448.9 24.7 all-gather.7
  482.5 35.4 reduce-scatter.4
where the time goes:
time: 529 us; the launch traced here: 526 us
  waiting for transfers between devices  241 us (46%)
  local copies, waits for them, and re-layouts  145 us (27%)
  other arithmetic  91.8 us (17%)
  matrix products  32.9 us (6%)
  between operations  13.4 us (3%)
    all_gather x1, waiting for transfers between devices, local(): arrived = lax.all_gather(prefix_cache, 'req', axis=0, tiled=True)  124 us
    dynamic_slice x96, local copies, waits for them, and re-layouts, local(): lax.scan(over_blocks, merged, (blocks, jnp.arange(block_count, dtype=jnp....  69.9 us
    reduce_sum x32, other arithmetic, lookup(): return jnp.sum(jnp.where(hits, values, 0))  42 us
    reshape x1, local copies, waits for them, and re-layouts, local(): blocks = arrived.reshape(block_count, block_rows, 2, head_count, HD)  41.4 us
    reduce_scatter x1, waiting for transfers between devices, feed_forward(): lax.psum_scatter(partial_sums.astype(jnp.bfloat16), 'mdl', scatter_dimens...  35.6 us
    reduce_scatter x1, waiting for transfers between devices, local(): lax.psum_scatter(head_terms.astype(jnp.bfloat16), 'mdl', scatter_dimensio...  32.8 us
    all_gather x1, waiting for transfers between devices, feed_forward(): full_rows = lax.all_gather(residual_rows, 'mdl', axis=1, tiled=True)  24.9 us
    all_gather x1, waiting for transfers between devices, local(): gathered = lax.all_gather(tokens, 'mdl', axis=1, tiled=True)  22.5 us
  transfers between devices with their start and end apart: 5, of which 5 were waited for; matrix products, arithmetic and copies ran while one was open for 5% of the time, Pallas kernels for 0%

commit v1 on v0

--- a/solution.py
+++ b/solution.py
@@ -132,7 +132,12 @@
     occupied, request, slot_group, offset, position = slot_table(
         lengths, placement, request_group, start_position, device, capacity
     )
-    gathered = lax.all_gather(tokens, "mdl", axis=1, tiled=True)
+    ring = [tokens]
+    for hop in range(7):
+        ring.append(lax.ppermute(ring[-1], "mdl", [(dev, (dev + 1) % 8) for dev in range(8)]))
+    gathered = jnp.roll(
+        jnp.concatenate(ring[::-1], axis=1), (lax.axis_index("mdl") + 1) * ring[0].shape[1], axis=1
+    )
     normed = layer_norm(gathered.astype(jnp.float32)).astype(jnp.bfloat16)
     projected = jnp.einsum("sd,dtc->stc", normed, qkv_weight, preferred_element_type=jnp.float32)
     queries = rotate(projected[:, 0].reshape(capacity, head_count, HD), position).astype(

time: 529 us -> 500 us (0.945)
  waiting for transfers between devices: 241 us -> 208 us
  local copies, waits for them, and re-layouts: 145 us -> 153 us
    all_gather x1, waiting for transfers between devices: 124 us -> 80.7 us  [local(): arrived = lax.all_gather(prefix_cache, 'req', axis=0, tiled=True)]
    ppermute x0 -> x7, waiting for transfers between devices: none -> 33.5 us  [local(): lax.ppermute(ring[-1], 'mdl', [(dev, (dev + 1) % 8) for dev in range(8)])]
    all_gather x1 -> x0, waiting for transfers between devices: 22.5 us -> none  [local(): gathered = lax.all_gather(tokens, 'mdl', axis=1, tiled=True)]
    unnamed x30 -> x51, local copies, waits for them, and re-layouts: 7.08 us -> 15.9 us
  transfers between devices with their start and end apart: 5 -> 11, of which waited for: 5 -> 11; matrix products, arithmetic and copies ran while one was open for 5% -> 6% of each run, Pallas kernels for 0% -> 0%
where the time goes in v1:
time: 500 us; the launch traced here: 497 us
  waiting for transfers between devices  208 us (42%)
  local copies, waits for them, and re-layouts  153 us (31%)
  other arithmetic  88 us (18%)
  matrix products  32 us (6%)
  between operations  13.5 us (3%)
    all_gather x1, waiting for transfers between devices, local(): arrived = lax.all_gather(prefix_cache, 'req', axis=0, tiled=True)  80.7 us
    dynamic_slice x96, local copies, waits for them, and re-layouts, local(): lax.scan(over_blocks, merged, (blocks, jnp.arange(block_count, dtype=jnp....  69.9 us
    reduce_sum x32, other arithmetic, lookup(): return jnp.sum(jnp.where(hits, values, 0))  42 us
    reshape x1, local copies, waits for them, and re-layouts, local(): blocks = arrived.reshape(block_count, block_rows, 2, head_count, HD)  41.4 us
    reduce_scatter x1, waiting for transfers between devices, feed_forward(): lax.psum_scatter(partial_sums.astype(jnp.bfloat16), 'mdl', scatter_dimens...  35.6 us
    ppermute x7, waiting for transfers between devices, local(): lax.ppermute(ring[-1], 'mdl', [(dev, (dev + 1) % 8) for dev in range(8)])  33.5 us
    reduce_scatter x1, waiting for transfers between devices, local(): lax.psum_scatter(head_terms.astype(jnp.bfloat16), 'mdl', scatter_dimensio...  32.9 us
    all_gather x1, waiting for transfers between devices, feed_forward(): full_rows = lax.all_gather(residual_rows, 'mdl', axis=1, tiled=True)  25 us
  transfers between devices with their start and end apart: 11, of which 11 were waited for; matrix products, arithmetic and copies ran while one was open for 6% of the time, Pallas kernels for 0%

profile of v1, /device:TPU:8, one launch (start us, length us, event | category | flops | bytes accessed | tf_op | source)
XLA Modules:
  0.0 497.3 jit_solution(1443835508242681260)
XLA Ops:
  8.1 5.0 %collective-permute-done = bf16[256,256]{1,0:T(8,128)(2,1)S(1)} collective-permute-done((bf16[256,256]{1,0:T(8,128)(2,1)}, bf16[256,256]{1,0:T(8,128)(2,1)S(1)}, u32[]{:S(2)}, u32[]{:S(2)}) %collective-permute-start) | collective-permute-done | bytes 131104 | tf_op jit(solution)/shard_map/ppermute | solution.py:137
  15.6 3.1 collective-permute-done.1
  18.8 5.6 %collective-permute-done.2 = bf16[256,256]{1,0:T(8,128)(2,1)S(1)} collective-permute-done((bf16[256,256]{1,0:T(8,128)(2,1)S(1)}, bf16[256,256]{1,0:T(8,128)(2,1)S(1)}, u32[]{:S(2)}, u32[]{:S(2)}) %collective-permute-start.2) | collective-permute-done | bytes 131104 | tf_op jit(solution)/shard_map/ppermute | solution.py:137
  25.7 4.3 collective-permute-done.3
  31.4 4.9 collective-permute-done.4
  37.4 4.8 collective-permute-done.5
  42.3 5.8 %collective-permute-done.6 = bf16[256,256]{1,0:T(8,128)(2,1)S(1)} collective-permute-done((bf16[256,256]{1,0:T(8,128)(2,1)}, bf16[256,256]{1,0:T(8,128)(2,1)S(1)}, u32[]{:S(2)}, u32[]{:S(2)}) %collective-permute-start.6) | collective-permute-done | bytes 131104 | tf_op jit(solution)/shard_map/ppermute | solution.py:137
  56.3 1.5 fusion.37
  59.9 1.7 copy.68
  61.6 1.7 fusion.77
  63.3 1.7 copy.66
  65.0 1.7 copy.67
  66.8 1.8 copy.65
  71.3 80.7 %all-gather.3.cloned.1.call-done = bf16[16384,2,256]{2,1,0:T(2,128)(2,1)} async-done(((bf16[512,2,256]{2,1,0:T(2,128)(2,1)}), bf16[16384,2,256]{2,1,0:T(2,128)(2,1)}) %all-gather.3.cloned.1.call-update) | async-done | bytes 16777232 | tf_op jit(solution)/shard_map/all_gather | solution.py:157
  152.0 41.4 %reshape.208 = bf16[32,512,2,2,128]{4,3,2,1,0:T(2,128)(2,1)} reshape(bf16[16384,2,256]{2,1,0:T(2,128)(2,1)} %all-gather.3.cloned.1.call-done) | data formatting | bytes 33554432 | tf_op jit(solution)/shard_map/reshape | solution.py:159
  193.4 188.9 %while.15 = (s32[]{:T(128)}, f32[256,2,128]{0,2,1:T(8,128)}, f32[256,2]{0,1:T(2,128)S(1)}, f32[256,2]{0,1:T(2,128)S(1)}, s32[32]{0:T(128)S(1)}, /*index=5*/s32[3...) while((s32[]{:T(128)}, f32[256,2,128]{0,2,1:T(8,128)}, ...), condition=%wide.region_13.14_spmd.clone, body=%wide.region_8.13_spmd.clone.sunk | while | flops 137171552 | bytes 8558420 | solution.py:168
  202.1 1.5 constant_dynamic-slice_fusion.2
  208.0 1.5 constant_dynamic-slice_fusion.2
  213.9 1.5 constant_dynamic-slice_fusion.2
  225.7 1.5 constant_dynamic-slice_fusion.2
  231.6 1.5 constant_dynamic-slice_fusion.2
  237.5 1.5 constant_dynamic-slice_fusion.2
  382.3 1.5 fusion.35
  385.4 32.9 %reduce-scatter.3.cloned.1.call-done = bf16[256,256]{1,0:T(8,128)(2,1)} async-done(((bf16[256,2048]{1,0:T(8,128)(2,1)}), bf16[256,256]{1,0:T(8,128)(2,1)}) %reduce-scatter.3.cloned.1.call-update) | async-done | bytes 131088 | tf_op jit(solution)/shard_map/reduce_scatter | solution.py:185
  418.2 1.6 add_convert_fusion
  419.9 25.0 %all-gather.5.cloned.1.call-done = bf16[256,2048]{1,0:T(8,128)(2,1)} async-done(((bf16[256,256]{1,0:T(8,128)(2,1)}), bf16[256,2048]{1,0:T(8,128)(2,1)}) %all-gather.5.cloned.1.call-update) | async-done | bytes 1048592 | tf_op jit(solution)/shard_map/all_gather | solution.py:104
  444.9 1.5 convert_reduce_fusion
  446.4 1.6 fusion.24
  448.1 3.7 fusion.18
  451.8 1.7 convolution_convert_fusion
  453.5 35.6 %reduce-scatter.5.cloned.1.call-done = bf16[256,256]{1,0:T(8,128)(2,1)} async-done(((bf16[256,2048]{1,0:T(8,128)(2,1)}), bf16[256,256]{1,0:T(8,128)(2,1)}) %reduce-scatter.5.cloned.1.call-update) | async-done | bytes 131088 | tf_op jit(solution)/shard_map/reduce_scatter | solution.py:109
  489.1 1.7 select_convert_fusion
  (570 shorter events, 200.7 us)
Async XLA Ops:
  6.5 49.8 %copy-start = (bf16[2048,3,256]{2,0,1:T(8,128)(2,1)S(1)}, bf16[2048,3,256]{2,0,1:T(8,128)(2,1)}, u32[]{:S(2)}) copy-start(bf16[2048,3,256]{2,0,1:T(8,128)(2,1)} %param.15) | copy-start | bytes 9437188
  6.5 47.1 %copy-start.3 = (bf16[256,256]{1,0:T(8,128)(2,1)S(1)}, bf16[256,256]{1,0:T(8,128)(2,1)}, u32[]{:S(2)}) copy-start(bf16[256,256]{1,0:T(8,128)(2,1)} %param.13) | copy-start | bytes 393220
  6.5 145.5 %all-gather.3.cloned.1.call-start = ((), (), s32[]{:S(2)}) async-start(), calls=%async_computation.2 | async-start | bytes 17301504 | tf_op jit(solution)/shard_map/all_gather | solution.py:157
  7.3 411.0 %reduce-scatter.3.cloned.1.call-start = ((), (), s32[]{:S(2)}) async-start(), calls=%async_computation.3 | async-start | bytes 1179648 | tf_op jit(solution)/shard_map/reduce_scatter | solution.py:185
  7.3 5.8 %collective-permute-start = (bf16[256,256]{1,0:T(8,128)(2,1)}, bf16[256,256]{1,0:T(8,128)(2,1)S(1)}, u32[]{:S(2)}, u32[]{:S(2)}) collective-permute-start(bf16[256,256]{1,0:T(8,128)(2,1)} %param.13), channel_id=1, source_target_pairs={{0,1},{1,2},{2,3},{3,4},{4,5},{5,6},{6,7},{7,0},{8,9},{9,10},{10,1... | collective-permute-start | bytes 393224 | tf_op jit(solution)/shard_map/ppermute | solution.py:137
  13.1 11.2 %copy-start.6 = (bf16[256,256]{1,0:T(8,128)(2,1)}, bf16[256,256]{1,0:T(8,128)(2,1)S(1)}, u32[]{:S(2)}) copy-start(bf16[256,256]{1,0:T(8,128)(2,1)S(1)} %collective-permute-done) | copy-start | bytes 393220
  13.1 5.6 %collective-permute-start.1 = (bf16[256,256]{1,0:T(8,128)(2,1)S(1)}, bf16[256,256]{1,0:T(8,128)(2,1)S(1)}, u32[]{:S(2)}, u32[]{:S(2)}) collective-permute-start(bf16[256,256]{1,0:T(8,128)(2,1)S(1)} %collective-permute-done), channel_id=1, source_target_pairs={{0,1},{1,2},{2,3},{3,4},{4,5},{5,6},{6,7},{7,0},{8,9},{9,10},{10,1... | collective-permute-start | bytes 393224 | tf_op jit(solution)/shard_map/ppermute | solution.py:137
  18.7 5.6 %copy-start.8 = (bf16[256,256]{1,0:T(8,128)(2,1)}, bf16[256,256]{1,0:T(8,128)(2,1)S(1)}, u32[]{:S(2)}) copy-start(bf16[256,256]{1,0:T(8,128)(2,1)S(1)} %collective-permute-done.1) | copy-start | bytes 393220
  18.7 5.6 %collective-permute-start.2 = (bf16[256,256]{1,0:T(8,128)(2,1)S(1)}, bf16[256,256]{1,0:T(8,128)(2,1)S(1)}, u32[]{:S(2)}, u32[]{:S(2)}) collective-permute-start(bf16[256,256]{1,0:T(8,128)(2,1)S(1)} %collective-permute-done.1), channel_id=1, source_target_pairs={{0,1},{1,2},{2,3},{3,4},{4,5},{5,6},{6,7},{7,0},{8,9},{9,10},{10,1... | collective-permute-start | bytes 393224 | tf_op jit(solution)/shard_map/ppermute | solution.py:137
  24.3 5.6 %collective-permute-start.3 = (bf16[256,256]{1,0:T(8,128)(2,1)S(1)}, bf16[256,256]{1,0:T(8,128)(2,1)S(1)}, u32[]{:S(2)}, u32[]{:S(2)}) collective-permute-start(bf16[256,256]{1,0:T(8,128)(2,1)S(1)} %collective-permute-done.2), channel_id=1, source_target_pairs={{0,1},{1,2},{2,3},{3,4},{4,5},{5,6},{6,7},{7,0},{8,9},{9,10},{10,1... | collective-permute-start | bytes 393224 | tf_op jit(solution)/shard_map/ppermute | solution.py:137
  30.6 5.7 %collective-permute-start.4 = (bf16[256,256]{1,0:T(8,128)(2,1)S(1)}, bf16[256,256]{1,0:T(8,128)(2,1)}, u32[]{:S(2)}, u32[]{:S(2)}) collective-permute-start(bf16[256,256]{1,0:T(8,128)(2,1)S(1)} %collective-permute-done.3), channel_id=1, source_target_pairs={{0,1},{1,2},{2,3},{3,4},{4,5},{5,6},{6,7},{7,0},{8,9},{9,10},{10,1... | collective-permute-start | bytes 393224 | tf_op jit(solution)/shard_map/ppermute | solution.py:137
  36.3 5.9 %collective-permute-start.5 = (bf16[256,256]{1,0:T(8,128)(2,1)}, bf16[256,256]{1,0:T(8,128)(2,1)}, u32[]{:S(2)}, u32[]{:S(2)}) collective-permute-start(bf16[256,256]{1,0:T(8,128)(2,1)} %collective-permute-done.4), channel_id=1, source_target_pairs={{0,1},{1,2},{2,3},{3,4},{4,5},{5,6},{6,7},{7,0},{8,9},{9,10},{10,1... | collective-permute-start | bytes 393224 | tf_op jit(solution)/shard_map/ppermute | solution.py:137
  36.5 18.9 %copy-start.13 = (bf16[256,256]{1,0:T(8,128)(2,1)S(1)}, bf16[256,256]{1,0:T(8,128)(2,1)}, u32[]{:S(2)}) copy-start(bf16[256,256]{1,0:T(8,128)(2,1)} %copy-done.12) | copy-start | bytes 393220
  36.6 19.0 %copy-start.11 = (bf16[256,256]{1,0:T(8,128)(2,1)S(1)}, bf16[256,256]{1,0:T(8,128)(2,1)}, u32[]{:S(2)}) copy-start(bf16[256,256]{1,0:T(8,128)(2,1)} %copy-done.10) | copy-start | bytes 393220
  36.6 19.0 %copy-start.9 = (bf16[256,256]{1,0:T(8,128)(2,1)S(1)}, bf16[256,256]{1,0:T(8,128)(2,1)}, u32[]{:S(2)}) copy-start(bf16[256,256]{1,0:T(8,128)(2,1)} %copy-done.8) | copy-start | bytes 393220
  36.6 19.0 %copy-start.7 = (bf16[256,256]{1,0:T(8,128)(2,1)S(1)}, bf16[256,256]{1,0:T(8,128)(2,1)}, u32[]{:S(2)}) copy-start(bf16[256,256]{1,0:T(8,128)(2,1)} %copy-done.6) | copy-start | bytes 393220
  42.2 5.8 %collective-permute-start.6 = (bf16[256,256]{1,0:T(8,128)(2,1)}, bf16[256,256]{1,0:T(8,128)(2,1)S(1)}, u32[]{:S(2)}, u32[]{:S(2)}) collective-permute-start(bf16[256,256]{1,0:T(8,128)(2,1)} %collective-permute-done.5), channel_id=1, source_target_pairs={{0,1},{1,2},{2,3},{3,4},{4,5},{5,6},{6,7},{7,0},{8,9},{9,10},{10,1... | collective-permute-start | bytes 393224 | tf_op jit(solution)/shard_map/ppermute | solution.py:137
  66.8 4.5 copy-start.14
  225.7 2.1 copy-start.16
  231.6 2.1 copy-start.16
  237.5 2.1 copy-start.16
  243.4 2.1 copy-start.16
  249.3 2.1 copy-start.16
  255.2 2.1 copy-start.16
  261.1 2.1 copy-start.16
  278.8 2.1 copy-start.16
  284.7 2.1 copy-start.16
  385.3 59.6 %all-gather.5.cloned.1.call-start = ((), (), s32[]{:S(2)}) async-start(), calls=%async_computation.4 | async-start | bytes 1179648 | tf_op jit(solution)/shard_map/all_gather | solution.py:104
  419.8 69.3 %reduce-scatter.5.cloned.1.call-start = ((), (), s32[]{:S(2)}) async-start(), calls=%async_computation.5 | async-start | bytes 1179648 | tf_op jit(solution)/shard_map/reduce_scatter | solution.py:109
  444.9 3.2 copy-start.1
  448.1 3.7 copy-start.15
  451.8 37.3 %copy-start.4 = (bf16[256,256]{1,0:T(8,128)(2,1)S(1)}, bf16[256,256]{1,0:T(8,128)(2,1)}, u32[]{:S(2)}) copy-start(bf16[256,256]{1,0:T(8,128)(2,1)} %add_convert_fusion) | copy-start | bytes 393220
  (59 other events, 74.6 us)
Sparse Core Ops, SparseCore 0:
  9.9 142.0 all-gather.2
  385.4 32.7 reduce-scatter.2
  420.1 24.7 all-gather.4
  453.7 35.4 reduce-scatter.4
